TPU v7x, 32 devices: a whole 2x2x4 slice. The times are simulated.
32 devices in a mesh: group: 4 (over x, core), replica: 8 (over z, y).
Axes of the slice: x: 2, y: 2, z: 4, core: 2. Of those that a mesh axis runs over, the one named last changes fastest.
Arguments:
- tokens: bfloat16 [16, 1024, 384], P('replica', 'group'), may hold values from -6 to 6
- cotangent: bfloat16 [16, 1024, 384], P('replica', 'group'), may hold values from -6 to 6
- weight: float32 [1774592], P('group'), may hold values from -1.6329932 to 1.6329932
- momentum: float32 [1774592], P('group'), may hold values from -40 to 40
- average: float32 [1774592], P('group'), may hold values from -1.6329932 to 1.6329932
- rate: float32 [1], replicated, may hold values from 0.00015625 to 0.000625
- step: int32 [1], replicated, may hold values from 1 to 20
Outputs:
- output: bfloat16 [16, 1024, 384], P('replica', 'group')
- grad_tokens: bfloat16 [16, 1024, 384], P('replica', 'group')
- grad: float32 [1774592], P('group')
- momentum_new: float32 [1774592], P('group')
- average_new: float32 [1774592], P('group')
- weight_new: float32 [1774592], P('group')
- weight_copy: bfloat16 [1774592], P('group')
All inputs are finite; a program needn't handle non-finite values.
Results may differ from a plain program's by a relative error of at most 0.013.
The roundings to bfloat16 on the way count: a program that leaves them out, or rounds other values in their place, can miss the bound.
Values may be sent and summed in bfloat16 or wider, within the bound.
No kernel may reach another device: no remote copies, remote signals or barrier semaphores. Data moves between devices by JAX's collectives and lax.ppermute only.
A program may use at most 448 MiB of HBM per device.

v0:
```python
from functools import partial
import jax
import jax.numpy as jnp
from jax import lax
from jax.sharding import PartitionSpec as P

D = 384
H = 6
DH = 64
FF = 1536
EPSILON = 1e-06
MOMENT = 0.9
DECAY_MAX = 0.999
INV_ROOT_TWO = 0.7071067811865476
INV_ROOT_TAU = 0.3989422804014327


def split_params(flat_vec):
    layout = (
        (D * 3 * D, (D, 3 * D)),
        (D * D, (D, D)),
        (D * FF, (D, FF)),
        (FF * D, (FF, D)),
        (D, (D,)),
        (D, (D,)),
        (3 * D, (3 * D,)),
        (DH, (DH,)),
        (DH, (DH,)),
        (D, (D,)),
        (D, (D,)),
        (D, (D,)),
        (FF, (FF,)),
        (D, (D,)),
    )
    pieces = []
    offset = 0
    for seg_len, seg_shape in layout:
        pieces.append(flat_vec[offset : offset + seg_len].reshape(seg_shape))
        offset = offset + seg_len
    return tuple(pieces)


def norm_forward(values, scale, shift):
    center = values - jnp.mean(values, -1, keepdims=True)
    inv_std = lax.rsqrt(jnp.mean(center * center, -1, keepdims=True) + EPSILON)
    normed = center * inv_std
    return (normed * scale + shift, normed, inv_std)


def norm_backward(grad_out, normed, inv_std, scale):
    grad_norm = grad_out * scale
    inner = jnp.mean(grad_norm * normed, -1, keepdims=True)
    return inv_std * (grad_norm - jnp.mean(grad_norm, -1, keepdims=True) - normed * inner)


def gelu_slope(values):
    return (
        0.5 * (1.0 + lax.erf(values * INV_ROOT_TWO))
        + values * jnp.exp(-0.5 * values * values) * INV_ROOT_TAU
    )


def cross_dot(left, right):
    return lax.dot_general(
        left, right, (((0,), (0,)), ((), ())), preferred_element_type=jnp.float32
    )


def back_dot(left, right):
    return lax.dot_general(
        left, right, (((1,), (1,)), ((), ())), preferred_element_type=jnp.float32
    )


def head_scores(query_b, key_block_rows, row_mask_values, scale_factor):
    query_masked = query_b * row_mask_values
    scores = (
        jnp.einsum("xuc,xlc->xul", query_masked, key_block_rows, preferred_element_type=jnp.float32)
        * scale_factor
    )
    return (query_masked, scores)


def attend_block(operands, masks, scale_factor):
    query_b, key_block_rows, value_block_rows = operands

    def attend_one_head(total, row_mask_values):
        query_masked, scores = head_scores(query_b, key_block_rows, row_mask_values, scale_factor)
        row_peak = jnp.max(scores, -1, keepdims=True)
        raised = jnp.exp(scores - row_peak)
        row_total = jnp.sum(raised, -1, keepdims=True)
        attention_weights = (raised / row_total).astype(jnp.bfloat16)
        part_out = jnp.einsum(
            "cxu,cuw->cxw",
            attention_weights,
            value_block_rows * row_mask_values,
            preferred_element_type=jnp.float32,
        )
        return (total + part_out, (row_peak + jnp.log(row_total))[..., 0])

    start = jnp.zeros(query_b.shape, jnp.float32)
    return lax.scan(attend_one_head, start, masks)


def head_grads(
    query_b, key_block_rows, value_block_rows, grad_b, log_h, inner_h, row_mask_values, scale_factor
):
    query_masked, scores = head_scores(query_b, key_block_rows, row_mask_values, scale_factor)
    probs = jnp.exp(scores - log_h[..., None])
    gradient_masked = grad_b * row_mask_values
    grad_probs = jnp.einsum(
        "xuc,xlc->xul", gradient_masked, value_block_rows, preferred_element_type=jnp.float32
    )
    inner_h = jnp.sum(probs * grad_probs, -1)
    score_gradient = (probs * (grad_probs - inner_h[..., None])).astype(jnp.bfloat16)
    return (probs, score_gradient, inner_h, query_masked, gradient_masked)


def local_back(operands, masks, scale_factor):
    query_b, key_block_rows, value_block_rows, grad_b, log_b = operands

    def local_one_head(carry, head_in):
        row_mask_values, log_h = head_in
        probs, score_gradient, inner_h, query_masked, gradient_masked = head_grads(
            query_b,
            key_block_rows,
            value_block_rows,
            grad_b,
            log_h,
            None,
            row_mask_values,
            scale_factor,
        )
        grad_query = (
            jnp.einsum(
                "cxu,cuw->cxw",
                score_gradient,
                key_block_rows * row_mask_values,
                preferred_element_type=jnp.float32,
            )
            * scale_factor
        )
        grad_key = (
            jnp.einsum(
                "fji,fjp->fip", score_gradient, query_masked, preferred_element_type=jnp.float32
            )
            * scale_factor
        )
        grad_value = jnp.einsum(
            "fji,fjp->fip",
            probs.astype(jnp.bfloat16),
            gradient_masked,
            preferred_element_type=jnp.float32,
        )
        return ((carry[0] + grad_query, carry[1] + grad_key, carry[2] + grad_value), None)

    start = (
        jnp.zeros(query_b.shape, jnp.float32),
        jnp.zeros(key_block_rows.shape, jnp.float32),
        jnp.zeros(key_block_rows.shape, jnp.float32),
    )
    totals, unused = lax.scan(local_one_head, start, (masks, log_b))
    return totals


def per_device(tokens, cotangent, weight, momentum, average, rate, step):
    image_count, own_len, width = tokens.shape
    row_count = image_count * own_len
    scale_factor = DH ** (-0.5)
    pair_size = 2
    head_masks = (
        lax.broadcasted_iota(jnp.int32, (H, width), 1) // DH
        == lax.broadcasted_iota(jnp.int32, (H, width), 0)
    ).astype(jnp.bfloat16)

    def in_blocks(array):
        return array.reshape((image_count // pair_size, pair_size) + array.shape[1:])

    def unblock(array):
        return array.reshape((image_count,) + array.shape[2:])

    shard_low = weight.astype(jnp.bfloat16)
    gathered = lax.all_gather(shard_low, "group", axis=0, tiled=True)
    (
        w_qkv,
        w_out,
        w_fc1,
        w_fc2,
        g_one,
        b_one,
        b_qkv,
        g_query,
        g_key,
        b_out,
        g_two,
        b_two,
        b_fc1,
        b_fc2,
    ) = split_params(gathered)
    (
        gain_one,
        bias_one,
        bias_qkv,
        gain_query,
        gain_key,
        bias_out,
        gain_two,
        bias_two,
        bias_fc1,
        bias_fc2,
    ) = tuple(
        (
            member.astype(jnp.float32)
            for member in (g_one, b_one, b_qkv, g_query, g_key, b_out, g_two, b_two, b_fc1, b_fc2)
        )
    )
    resid_in = tokens.astype(jnp.float32).reshape(row_count, width)
    ln_one_out, normed_one, inv_one = norm_forward(resid_in, gain_one, bias_one)
    act_one = ln_one_out.astype(jnp.bfloat16)
    qkv_full = jnp.dot(act_one, w_qkv, preferred_element_type=jnp.float32) + bias_qkv
    head_shape = (row_count, H, DH)
    query_pre = qkv_full[:, :width].reshape(head_shape)
    key_pre = qkv_full[:, width : 2 * width].reshape(head_shape)
    value_pre = qkv_full[:, 2 * width :]
    query_out, query_normed, query_inv = norm_forward(query_pre, gain_query, 0.0)
    key_out, key_normed, key_inv = norm_forward(key_pre, gain_key, 0.0)
    image_shape = (image_count, own_len, width)
    query_low = query_out.astype(jnp.bfloat16).reshape(image_shape)
    key_low = key_out.astype(jnp.bfloat16).reshape(image_shape)
    value_low = value_pre.astype(jnp.bfloat16).reshape(image_shape)
    key_all, value_all = (
        lax.all_gather(key_low, "group", axis=1, tiled=True),
        lax.all_gather(value_low, "group", axis=1, tiled=True),
    )
    attn_out, log_sum = lax.map(
        partial(attend_block, masks=head_masks, scale_factor=scale_factor),
        (in_blocks(query_low), in_blocks(key_all), in_blocks(value_all)),
    )
    attn_low = unblock(attn_out).reshape(row_count, width).astype(jnp.bfloat16)
    resid_mid = resid_in + jnp.dot(attn_low, w_out, preferred_element_type=jnp.float32) + bias_out
    ln_two_out, normed_two, inv_two = norm_forward(resid_mid, gain_two, bias_two)
    act_two = ln_two_out.astype(jnp.bfloat16)
    hidden_pre = jnp.dot(act_two, w_fc1, preferred_element_type=jnp.float32) + bias_fc1
    hidden_low = jax.nn.gelu(hidden_pre, approximate=False).astype(jnp.bfloat16)
    result = resid_mid + jnp.dot(hidden_low, w_fc2, preferred_element_type=jnp.float32) + bias_fc2
    out_tokens = result.astype(jnp.bfloat16).reshape(tokens.shape)
    regathered = lax.all_gather(shard_low, "group", axis=0, tiled=True)
    back_qkv, back_out, back_fc1, back_fc2 = split_params(regathered)[:4]
    grad_res = cotangent.astype(jnp.float32).reshape(row_count, width)
    grad_mlp = cotangent.reshape(row_count, width)
    d_bias_fc2 = jnp.sum(grad_res, 0)
    d_w_fc2 = cross_dot(hidden_low, grad_mlp)
    grad_pre = (back_dot(grad_mlp, back_fc2) * gelu_slope(hidden_pre)).astype(jnp.bfloat16)
    d_bias_fc1 = jnp.sum(grad_pre.astype(jnp.float32), 0)
    d_w_fc1 = cross_dot(act_two, grad_pre)
    grad_norm_two = back_dot(grad_pre, back_fc1)
    d_gain_two = jnp.sum(grad_norm_two * normed_two, 0)
    d_bias_two = jnp.sum(grad_norm_two, 0)
    grad_mid = grad_res + norm_backward(grad_norm_two, normed_two, inv_two, gain_two)
    grad_proj = grad_mid.astype(jnp.bfloat16)
    d_bias_out = jnp.sum(grad_proj.astype(jnp.float32), 0)
    d_w_out = cross_dot(attn_low, grad_proj)
    grad_attn = back_dot(grad_proj, back_out).astype(jnp.bfloat16).reshape(image_shape)
    grad_q, grad_k_all, grad_v_all = lax.map(
        partial(local_back, masks=head_masks, scale_factor=scale_factor),
        (
            in_blocks(query_low),
            in_blocks(key_all),
            in_blocks(value_all),
            in_blocks(grad_attn),
            log_sum,
        ),
    )
    grad_key, grad_value = (
        lax.psum_scatter(
            unblock(grad_k_all).astype(jnp.bfloat16), "group", scatter_dimension=1, tiled=True
        ).astype(jnp.float32),
        lax.psum_scatter(
            unblock(grad_v_all).astype(jnp.bfloat16), "group", scatter_dimension=1, tiled=True
        ).astype(jnp.float32),
    )
    grad_query_n = unblock(grad_q).reshape(head_shape).astype(jnp.bfloat16).astype(jnp.float32)
    grad_key_n = grad_key.reshape(head_shape).astype(jnp.bfloat16).astype(jnp.float32)
    grad_value_n = grad_value.reshape(row_count, width).astype(jnp.bfloat16).astype(jnp.float32)
    d_gain_query = jnp.sum(grad_query_n * query_normed, (0, 1))
    d_gain_key = jnp.sum(grad_key_n * key_normed, (0, 1))
    grad_query_pre = norm_backward(grad_query_n, query_normed, query_inv, gain_query).reshape(
        row_count, width
    )
    grad_key_pre = norm_backward(grad_key_n, key_normed, key_inv, gain_key).reshape(
        row_count, width
    )
    grad_qkv = jnp.concatenate([grad_query_pre, grad_key_pre, grad_value_n], 1).astype(jnp.bfloat16)
    d_bias_qkv = jnp.sum(grad_qkv.astype(jnp.float32), 0)
    d_w_qkv = cross_dot(act_one, grad_qkv)
    grad_norm_one = back_dot(grad_qkv, back_qkv)
    d_gain_one = jnp.sum(grad_norm_one * normed_one, 0)
    d_bias_one = jnp.sum(grad_norm_one, 0)
    grad_in = grad_mid + norm_backward(grad_norm_one, normed_one, inv_one, gain_one)
    grad_tokens = grad_in.astype(jnp.bfloat16).reshape(tokens.shape)
    local_grad = jnp.concatenate(
        [
            member.reshape(-1)
            for member in (
                d_w_qkv,
                d_w_out,
                d_w_fc1,
                d_w_fc2,
                d_gain_one,
                d_bias_one,
                d_bias_qkv,
                d_gain_query,
                d_gain_key,
                d_bias_out,
                d_gain_two,
                d_bias_two,
                d_bias_fc1,
                d_bias_fc2,
            )
        ]
    )
    group_grad = lax.psum_scatter(
        local_grad.astype(jnp.bfloat16), "group", scatter_dimension=0, tiled=True
    ).astype(jnp.float32)
    grad_total = lax.psum(group_grad, "replica")
    momentum_new = MOMENT * momentum + grad_total
    weight_new = weight - rate[0] * (grad_total + MOMENT * momentum_new)
    step_value = step[0].astype(jnp.float32)
    ema_decay = jnp.minimum(DECAY_MAX, (1.0 + step_value) / (10.0 + step_value))
    average_new = ema_decay * average + (1.0 - ema_decay) * weight_new
    return (
        out_tokens,
        grad_tokens,
        grad_total,
        momentum_new,
        average_new,
        weight_new,
        weight_new.astype(jnp.bfloat16),
    )


def solution(mesh):
    in_specs = (
        P("replica", "group", None),
        P("replica", "group", None),
        P("group"),
        P("group"),
        P("group"),
        P(),
        P(),
    )
    out_specs = (
        P("replica", "group", None),
        P("replica", "group", None),
        P("group"),
        P("group"),
        P("group"),
        P("group"),
        P("group"),
    )
    return jax.shard_map(
        per_device, mesh=mesh, in_specs=in_specs, out_specs=out_specs, check_vma=False
    )
```

profile of v0, /device:TPU:0, one launch (start us, length us, event | category | flops | bytes accessed | tf_op | source)
XLA Modules:
  0.0 935.1 jit_solution(8608521233848531671)
XLA Ops:
  8.8 10.9 %reshape.335 = bf16[1,1,443648]{2,1,0:T(2,128)(2,1)} reshape(bf16[443648]{0:T(1024)(128)(2,1)S(1)} %convert_element_type.177) | data formatting | bytes 1774592
  21.7 51.8 %all-gather.9.cloned.1.call-done = bf16[4,1,443648]{2,1,0:T(2,128)(2,1)} async-done(((bf16[1,1,443648]{2,1,0:T(2,128)(2,1)}), bf16[4,1,443648]{2,1,0:T(2,128)(2,1)}) %all-gather.9.cloned.1.call-update) | async-done | bytes 3549200 | tf_op jit(solution)/shard_map/all_gather | solution.py:183
  73.5 78.3 %reduce.13 = bf16[4,443648]{1,0:T(4,128)(2,1)} reduce(bf16[4,1,443648]{2,1,0:T(2,128)(2,1)} %all-gather.9.cloned.1.call-done, bf16[]{:T(256)} %constant.199), dimensions={1}, to_apply=%all-gather.reduce_sub_computation | reduce | bytes 7098370 | tf_op jit(solution)/shard_map/all_gather | solution.py:183
  151.8 3.3 reshape.336
  159.8 2.9 reshape.314
  172.9 2.5 mul.382
  178.0 3.3 multiply_convert_fusion.1
  182.8 3.2 fusion.70
  186.3 3.2 reshape.322
  196.5 2.9 multiply_convert_fusion.2
  201.5 3.7 copy.71
  205.2 17.9 %all-gather.7.cloned.1.call-done = bf16[2,1024,384]{2,1,0:T(8,128)(2,1)} async-done(((bf16[2,256,384]{2,1,0:T(8,128)(2,1)}), bf16[2,1024,384]{2,1,0:T(8,128)(2,1)}) %all-gather.7.cloned.1.call-update) | async-done | bytes 1572880 | tf_op jit(solution)/shard_map/all_gather | solution.py:233
  223.1 15.4 %while.48 = (s32[]{:T(128)}, f32[2,256,384]{2,1,0:T(8,128)S(1)}, f32[6,2,256]{2,1,0:T(2,128)S(1)}, bf16[6,384]{1,0:T(8,128)(2,1)S(1)}, bf16[2,256,384]{2,1,0:T(8...) while((s32[]{:T(128)}, f32[2,256,384]{2,1,0:T(8,128)S(1)}, ...), condition=%wide.region_9.10_spmd.clone, body=%wide.region_6.9_spmd.clone.sunk | while | flops 811400704 | bytes 17714324 | solution.py:102
  240.0 8.8 fusion.34
  255.1 70.3 %while.49 = (s32[]{:T(128)}, f32[2,256,384]{2,1,0:T(8,128)}, f32[2,1024,384]{2,1,0:T(8,128)}, f32[2,1024,384]{2,1,0:T(8,128)}, bf16[6,384]{1,0:T(8,128)(2,1)S(1)...) while((s32[]{:T(128)}, f32[2,256,384]{2,1,0:T(8,128)}, ...), condition=%wide.region_16.17_spmd.clone, body=%wide.region_14.16_spmd.clone.sunk | while | flops 2023554560 | bytes 92814896 | solution.py:162
  327.5 61.8 %copy.90 = bf16[2,1024,384]{0,2,1:T(8,128)(2,1)} copy(bf16[2,1024,384]{2,1,0:T(8,128)(2,1)S(1)} %convert_element_type.230) | data formatting | bytes 3145728
  389.2 162.7 %reshape.337 = bf16[1024,768]{1,0:T(8,128)(2,1)} reshape(bf16[1024,384,2]{2,1,0:T(8,128)(2,1)} %bitcast.29) | data formatting | bytes 3145728
  570.6 3.5 convolution_convert_fusion.1
  574.1 3.7 reshape.329
  577.8 3.1 multiply_reduce_fusion.4
  586.1 56.0 %reshape.338 = bf16[256,384,2]{2,1,0:T(8,128)(2,1)} reshape(bf16[256,768]{1,0:T(8,128)(2,1)} %reduce-scatter.7.cloned.1.call-done) | data formatting | bytes 786432
  642.1 23.3 %copy.91 = bf16[2,256,384]{1,0,2:T(2,128)(2,1)S(1)} copy(bf16[2,256,384]{0,2,1:T(8,128)(2,1)} %bitcast.123) | data formatting | bytes 786432
  667.9 3.1 multiply_reduce_fusion.3
  680.4 4.6 fusion.57
  686.5 4.0 multiply_reduce_fusion.5
  692.1 2.8 reshape.327
  694.9 50.5 %concatenate.9 = bf16[1774592]{0:T(1024)(128)(2,1)} concatenate(bf16[442368]{0:T(1024)(128)(2,1)} %reshape.327, bf16[147456]{0:T(1024)(128)(2,1)} %reshape.328, bf16[589824]{0:T(1024)(128)(2,1)S(1)} %copy-done.38, bf16[589824]{0:T(1024)(128)(2,1)S(1)} %copy-done.37, bf16[384]{0:T(512)(128)(2,1)} %get-tuple-element.265, bf16[384]{0:T(512)(128)(2,1)} %get-tuple-element.274, ...), dimensions={0} | concatenate | bytes 7098368 | tf_op jit(solution)/shard_map/concatenate | solution.py:301
  747.3 73.6 %all-reduce.6.cloned.1.call-done = bf16[1774592]{0:T(1024)(128)(2,1)} async-done(((bf16[1774592]{0:T(1024)(128)(2,1)}), bf16[1774592]{0:T(1024)(128)(2,1)}) %all-reduce.6.cloned.1.call-update) | async-done | bytes 3549200
  820.9 2.9 dynamic-slice_convert_fusion
  825.2 3.2 fusion.49
  829.6 90.3 %all-reduce.4.cloned.1.call-done = f32[443648]{0:T(1024)} async-done(((f32[443648]{0:T(1024)}), f32[443648]{0:T(1024)}) %all-reduce.4.cloned.1.call-update) | async-done | bytes 1774608 | tf_op jit(solution)/shard_map/psum | solution.py:325
  919.8 4.0 fusion.69
  (436 shorter events, 171.3 us)
Async XLA Ops:
  7.2 66.3 %all-gather.9.cloned.1.call-start = ((), (), s32[]{:S(2)}) async-start(), calls=%async_computation.6 | async-start | bytes 8872960 | tf_op jit(solution)/shard_map/all_gather | solution.py:183
  8.8 11.0 %copy-start.15 = (bf16[2,256,384]{2,1,0:T(8,128)(2,1)S(1)}, bf16[2,256,384]{2,1,0:T(8,128)(2,1)}, u32[]{:S(2)}) copy-start(bf16[2,256,384]{2,1,0:T(8,128)(2,1)} %param.11) | copy-start | bytes 1179652
  19.7 181.8 %all-gather.5.cloned.1.call-start = ((), (), s32[]{:S(2)}) async-start(), calls=%async_computation.2 | async-start | bytes 1966080 | tf_op jit(solution)/shard_map/all_gather | solution.py:232
  155.1 8.7 copy-start.8
  159.8 18.2 %copy-start.60 = (f32[384]{0:T(512)}, f32[384]{0:T(512)S(1)}, u32[]{:S(2)}) copy-start(f32[384]{0:T(512)S(1)} %mul.385) | copy-start | bytes 4612
  165.9 16.0 %copy-start.6 = (f32[512,1152]{1,0:T(8,128)}, f32[512,1152]{1,0:T(8,128)S(1)}, u32[]{:S(2)}) copy-start(f32[512,1152]{1,0:T(8,128)S(1)} %convolution_add_fusion) | copy-start | bytes 7077892
  171.1 6.9 copy-start.54
  178.0 8.0 copy-start.32
  181.4 41.8 %all-gather.7.cloned.1.call-start = ((), (), s32[]{:S(2)}) async-start(), calls=%async_computation.3 | async-start | bytes 1966080 | tf_op jit(solution)/shard_map/all_gather | solution.py:233
  182.7 403.4 %reduce-scatter.7.cloned.1.call-start = ((), (), s32[]{:S(2)}) async-start(), calls=%async_computation.7 | async-start | bytes 1966080
  186.1 9.4 %copy-start.62 = (f32[384]{0:T(512)}, f32[384]{0:T(512)S(1)}, u32[]{:S(2)}) copy-start(f32[384]{0:T(512)S(1)} %mul.377) | copy-start | bytes 4612
  199.4 23.8 %copy-start.51 = (f32[2,256,384]{2,1,0:T(8,128)S(1)}, f32[2,256,384]{2,1,0:T(8,128)}, u32[]{:S(2)}) copy-start(f32[2,256,384]{2,1,0:T(8,128)} %custom-call) | copy-start | bytes 2359300
  223.1 15.6 %copy-start.16 = (bf16[2,256,384]{2,1,0:T(8,128)(2,1)S(1)}, bf16[2,256,384]{2,1,0:T(8,128)(2,1)}, u32[]{:S(2)}) copy-start(bf16[2,256,384]{2,1,0:T(8,128)(2,1)} %param.11) | copy-start | bytes 1179652
  223.1 15.6 %copy-start.67 = (f32[384]{0:T(512)S(1)}, f32[384]{0:T(512)}, u32[]{:S(2)}) copy-start(f32[384]{0:T(512)} %get-tuple-element.321) | copy-start | bytes 4612
  239.4 13.4 %copy-start.21 = (f32[512,384]{1,0:T(8,128)}, f32[512,384]{1,0:T(8,128)S(1)}, u32[]{:S(2)}) copy-start(f32[512,384]{1,0:T(8,128)S(1)} %get-tuple-element.338) | copy-start | bytes 2359300
  240.0 8.8 copy-start.45
  240.0 8.8 copy-start.46
  389.2 163.4 %copy-start.68 = (f32[1,2,2,128]{3,2,1,0:T(2,128)S(1)}, f32[1,2,2,128]{3,2,1,0:T(2,128)}, u32[]{:S(2)}) copy-start(f32[1,2,2,128]{3,2,1,0:T(2,128)} %get-tuple-element.335) | copy-start | bytes 6148
  389.2 164.0 %copy-start.69 = (f32[1,2,2,128]{3,2,1,0:T(2,128)S(1)}, f32[1,2,2,128]{3,2,1,0:T(2,128)}, u32[]{:S(2)}) copy-start(f32[1,2,2,128]{3,2,1,0:T(2,128)} %get-tuple-element.333) | copy-start | bytes 6148
  552.0 133.1 %reduce-scatter.5.cloned.1.call-start = ((), (), s32[]{:S(2)}) async-start(), calls=%async_computation.4 | async-start | bytes 1966080 | tf_op jit(solution)/shard_map/reduce_scatter | solution.py:278
  565.1 255.8 %all-reduce.6.cloned.1.call-start = ((), (), s32[]{:S(2)}) async-start(), calls=%async_computation.8 | async-start | bytes 7098368
  570.6 7.2 copy-start.34
  570.6 7.2 copy-start.35
  574.1 8.1 copy-start.12
  574.1 8.1 copy-start.57
  665.4 6.9 copy-start.10
  665.4 6.9 copy-start.55
  745.4 79.7 %copy-start.23 = (f32[512,384]{1,0:T(8,128)S(1)}, f32[512,384]{1,0:T(8,128)}, u32[]{:S(2)}) copy-start(f32[512,384]{1,0:T(8,128)} %copy-done.21) | copy-start | bytes 2359300
  745.4 79.7 %copy-start.47 = (bf16[1536,384]{1,0:T(8,128)(2,1)S(1)}, bf16[1536,384]{1,0:T(8,128)(2,1)}, u32[]{:S(2)}) copy-start(bf16[1536,384]{1,0:T(8,128)(2,1)} %reshape.322) | copy-start | bytes 3538948
  745.5 79.7 %copy-start.77 = (f32[384]{0:T(512)S(1)}, f32[384]{0:T(512)}, u32[]{:S(2)}) copy-start(f32[384]{0:T(512)} %get-tuple-element.318) | copy-start | bytes 4612
  745.5 174.4 %all-reduce.4.cloned.1.call-start = ((), (), s32[]{:S(2)}) async-start(), calls=%async_computation.5 | async-start | bytes 3555328 | tf_op jit(solution)/shard_map/psum | solution.py:325
  828.4 91.5 %copy-start.20 = (f32[443648]{0:T(1024)S(1)}, f32[443648]{0:T(1024)}, u32[]{:S(2)}) copy-start(f32[443648]{0:T(1024)} %param.13) | copy-start | bytes 5323780
  (94 other events, 243.8 us)
Sparse Core Ops, SparseCore 0:
  19.8 53.6 all-gather.8
  181.5 19.8 all-gather.4
  203.5 19.6 all-gather.6
  552.1 28.0 reduce-scatter.6
  583.1 28.0 reduce-scatter.4
  745.6 75.2 all-reduce.5
  825.1 94.7 all-reduce.3
where the time goes:
time: 944 us; the launch traced here: 935 us
  local copies, waits for them, and re-layouts  471 us (50%)
  waiting for transfers between devices  234 us (25%)
  other arithmetic  128 us (14%)
  matrix products  83.4 us (9%)
  between operations  17.3 us (2%)
    unnamed x164, local copies, waits for them, and re-layouts  332 us
    psum x1, waiting for transfers between devices, per_device(): grad_total = lax.psum(group_grad, 'replica')  90.3 us
    all_gather x1, other arithmetic, per_device(): gathered = lax.all_gather(shard_low, 'group', axis=0, tiled=True)  78.3 us
    unnamed x9, waiting for transfers between devices  73.7 us
    all_gather x1, waiting for transfers between devices, per_device(): gathered = lax.all_gather(shard_low, 'group', axis=0, tiled=True)  51.8 us
    concatenate x1, local copies, waits for them, and re-layouts, per_device(): jnp.concatenate([member.reshape(-1) for member in (d_w_qkv, d_w_out, d_w_...  50.5 us
    while x84, local copies, waits for them, and re-layouts  27.4 us
  transfers between devices with their start and end apart: 7, of which 4 were waited for; matrix products, arithmetic and copies ran while one was open for 17% of the time, Pallas kernels for 0%

commit v1 on v0

--- a/solution.py
+++ b/solution.py
@@ -13,6 +13,24 @@
 DECAY_MAX = 0.999
 INV_ROOT_TWO = 0.7071067811865476
 INV_ROOT_TAU = 0.3989422804014327
+
+
+def laid_out(parts, dim):
+    shape = list(parts.shape[1:])
+    shape[dim] *= parts.shape[0]
+    return jnp.moveaxis(parts, 0, dim).reshape(shape)
+
+
+def grow_blocks(shard, axis):
+    devices = lax.axis_size(axis)
+    blocks = shard[None]
+    for level in range(devices.bit_length() - 1):
+        apart = 1 << level
+        theirs = lax.ppermute(blocks, axis, [(i, i ^ apart) for i in range(devices)])
+        both = jnp.stack([blocks, theirs])
+        upper = lax.axis_index(axis) >> level & 1
+        blocks = jnp.where(upper == 0, both, both[::-1]).reshape(-1, *shard.shape)
+    return blocks
 
 
 def split_params(flat_vec):
@@ -180,7 +198,7 @@
         return array.reshape((image_count,) + array.shape[2:])
 
     shard_low = weight.astype(jnp.bfloat16)
-    gathered = lax.all_gather(shard_low, "group", axis=0, tiled=True)
+    gathered = laid_out(grow_blocks(shard_low, "group"), 0)
     (
         w_qkv,
         w_out,

time: 944 us -> 1030 us (1.091)
  local copies, waits for them, and re-layouts: 471 us -> 511 us
  other arithmetic: 128 us -> 154 us
  waiting for transfers between devices: 234 us -> 247 us
    ppermute x0 -> x2, waiting for transfers between devices: none -> 37.9 us  [grow_blocks(): lax.ppermute(blocks, axis, [(i, i ^ apart) for i in range(devices)])]
    all_gather x1, waiting for transfers between devices: 51.8 us -> 23.4 us  [per_device(): regathered = lax.all_gather(shard_low, 'group', axis=0, tiled=True)]
    another operation x0 -> x2, local copies, waits for them, and re-layouts: none -> 14.3 us  [the longest x1 10.1 us: grow_blocks(): both = jnp.stack([blocks, theirs])]
    another operation x2 -> x4, other arithmetic: 4.61 us -> 17.5 us  [the longest x2 12.9 us: grow_blocks(): both = jnp.stack([blocks, theirs])]
    broadcast_in_dim x0 -> x1, local copies, waits for them, and re-layouts: none -> 10.9 us  [grow_blocks(): blocks = shard[None]]
    select_n x0 -> x2, other arithmetic: none -> 10.4 us  [grow_blocks(): blocks = jnp.where(upper == 0, both, both[::-1]).reshape(-1, *shard.shape)]
    unnamed x164 -> x174, local copies, waits for them, and re-layouts: 332 us -> 328 us
  transfers between devices with their start and end apart: 7 -> 9, of which waited for: 4 -> 6; matrix products, arithmetic and copies ran while one was open for 17% -> 20% of each run, Pallas kernels for 0% -> 0%
where the time goes in v1:
time: 1030 us; the launch traced here: 1020 us
  local copies, waits for them, and re-layouts  511 us (50%)
  waiting for transfers between devices  247 us (24%)
  other arithmetic  154 us (15%)
  matrix products  85.8 us (8%)
  between operations  17.4 us (2%)
    unnamed x174, local copies, waits for them, and re-layouts  328 us
    psum x1, waiting for transfers between devices, per_device(): grad_total = lax.psum(group_grad, 'replica')  88.5 us
    all_gather x1, other arithmetic, per_device(): regathered = lax.all_gather(shard_low, 'group', axis=0, tiled=True)  78.3 us
    unnamed x9, waiting for transfers between devices  74.4 us
    concatenate x1, local copies, waits for them, and re-layouts, per_device(): jnp.concatenate([member.reshape(-1) for member in (d_w_qkv, d_w_out, d_w_...  50.4 us
    ppermute x2, waiting for transfers between devices, grow_blocks(): lax.ppermute(blocks, axis, [(i, i ^ apart) for i in range(devices)])  37.9 us
    while x84, local copies, waits for them, and re-layouts  28.4 us
    all_gather x1, waiting for transfers between devices, per_device(): regathered = lax.all_gather(shard_low, 'group', axis=0, tiled=True)  23.4 us
  transfers between devices with their start and end apart: 9, of which 6 were waited for; matrix products, arithmetic and copies ran while one was open for 20% of the time, Pallas kernels for 0%

profile of v1, /device:TPU:0, one launch (start us, length us, event | category | flops | bytes accessed | tf_op | source)
XLA Modules:
  0.0 1019.1 jit_solution(11322637822011364521)
XLA Ops:
  8.8 10.9 %broadcast_in_dim.13 = bf16[1,443648]{1,0:T(2,128)(2,1)} reshape(bf16[443648]{0:T(1024)(128)(2,1)S(1)} %convert_element_type.177) | data formatting | bytes 1774592 | tf_op jit(solution)/shard_map/broadcast_in_dim | solution.py:26
  20.2 10.1 stack_broadcast_in_dim.3
  30.3 6.0 pad_maximum_fusion
  36.3 5.6 broadcast_select_fusion
  41.9 5.8 copy.124
  51.8 37.9 %collective-permute-done.1 = bf16[2,443648]{1,0:T(2,128)(2,1)} collective-permute-done((bf16[2,443648]{1,0:T(2,128)(2,1)S(1)}, bf16[2,443648]{1,0:T(2,128)(2,1)}, u32[]{:S(2)}, u32[]{:S(2)}) %collective-permute-start.1) | collective-permute-done | bytes 1774624 | tf_op jit(solution)/shard_map/ppermute | solution.py:29
  89.7 6.9 pad_maximum_fusion.1
  96.6 4.8 broadcast_select_fusion.1
  101.4 4.2 reshape_reshape.2
  149.0 4.8 all-gather.5.cloned.1.call-done
  153.8 3.7 copy.95
  157.6 18.1 %all-gather.7.cloned.1.call-done = bf16[2,1024,384]{2,1,0:T(8,128)(2,1)} async-done(((bf16[2,256,384]{2,1,0:T(8,128)(2,1)}), bf16[2,1024,384]{2,1,0:T(8,128)(2,1)}) %all-gather.7.cloned.1.call-update) | async-done | bytes 1572880 | tf_op jit(solution)/shard_map/all_gather | solution.py:251
  175.6 19.3 %while.48 = (s32[]{:T(128)}, f32[2,256,384]{2,1,0:T(8,128)S(1)}, f32[6,2,256]{2,1,0:T(2,128)}, bf16[6,384]{1,0:T(8,128)(2,1)S(1)}, bf16[2,256,384]{2,1,0:T(8,128...) while((s32[]{:T(128)}, f32[2,256,384]{2,1,0:T(8,128)S(1)}, ...), condition=%wide.region_9.10_spmd.clone, body=%wide.region_6.9_spmd.clone.sunk | while | flops 811400704 | bytes 17714324 | solution.py:120
  196.3 9.0 fusion.34
  205.3 23.4 %all-gather.9.cloned.1.call-done = bf16[4,1,443648]{2,1,0:T(2,128)(2,1)} async-done(((bf16[1,1,443648]{2,1,0:T(2,128)(2,1)}), bf16[4,1,443648]{2,1,0:T(2,128)(2,1)}) %all-gather.9.cloned.1.call-update) | async-done | bytes 3549200 | tf_op jit(solution)/shard_map/all_gather | solution.py:265
  228.7 78.3 %reduce.13 = bf16[4,443648]{1,0:T(4,128)(2,1)} reduce(bf16[4,1,443648]{2,1,0:T(2,128)(2,1)} %all-gather.9.cloned.1.call-done, bf16[]{:T(256)} %constant.205), dimensions={1}, to_apply=%all-gather.reduce_sub_computation | reduce | bytes 7098370 | tf_op jit(solution)/shard_map/all_gather | solution.py:265
  307.0 5.1 reshape.352
  316.2 3.5 reshape.339
  322.8 4.3 fusion.74
  330.9 74.9 %while.49 = (s32[]{:T(128)}, f32[2,256,384]{2,1,0:T(8,128)}, f32[2,1024,384]{2,1,0:T(8,128)}, f32[2,1024,384]{2,1,0:T(8,128)}, bf16[6,384]{1,0:T(8,128)(2,1)S(1)...) while((s32[]{:T(128)}, f32[2,256,384]{2,1,0:T(8,128)}, ...), condition=%wide.region_16.17_spmd.clone, body=%wide.region_14.16_spmd.clone.sunk | while | flops 2023554560 | bytes 92814896 | solution.py:180
  407.9 61.9 %copy.114 = bf16[2,1024,384]{0,2,1:T(8,128)(2,1)} copy(bf16[2,1024,384]{2,1,0:T(8,128)(2,1)S(1)} %convert_element_type.230) | data formatting | bytes 3145728
  469.8 162.7 %reshape.353 = bf16[1024,768]{1,0:T(8,128)(2,1)} reshape(bf16[1024,384,2]{2,1,0:T(8,128)(2,1)} %bitcast.31) | data formatting | bytes 3145728
  658.1 3.7 reshape.345
  670.1 56.0 %reshape.354 = bf16[256,384,2]{2,1,0:T(8,128)(2,1)} reshape(bf16[256,768]{1,0:T(8,128)(2,1)} %reduce-scatter.7.cloned.1.call-done) | data formatting | bytes 786432
  726.1 23.3 %copy.115 = bf16[2,256,384]{1,0,2:T(2,128)(2,1)S(1)} copy(bf16[2,256,384]{0,2,1:T(8,128)(2,1)} %bitcast.130) | data formatting | bytes 786432
  764.5 4.6 fusion.57
  770.6 4.0 multiply_reduce_fusion.5
  779.1 50.4 %concatenate.9 = bf16[1774592]{0:T(1024)(128)(2,1)} concatenate(bf16[442368]{0:T(1024)(128)(2,1)} %reshape.343, bf16[147456]{0:T(1024)(128)(2,1)} %reshape.344, bf16[589824]{0:T(1024)(128)(2,1)S(1)} %copy-done.38, bf16[589824]{0:T(1024)(128)(2,1)S(1)} %copy-done.37, bf16[384]{0:T(512)(128)(2,1)} %get-tuple-element.282, bf16[384]{0:T(512)(128)(2,1)} %get-tuple-element.291, ...), dimensions={0} | concatenate | bytes 7098368 | tf_op jit(solution)/shard_map/concatenate | solution.py:319
  831.4 73.6 %all-reduce.6.cloned.1.call-done = bf16[1774592]{0:T(1024)(128)(2,1)} async-done(((bf16[1774592]{0:T(1024)(128)(2,1)}), bf16[1774592]{0:T(1024)(128)(2,1)}) %all-reduce.6.cloned.1.call-update) | async-done | bytes 3549200
  910.7 3.5 fusion.49
  915.4 88.5 %all-reduce.4.cloned.1.call-done = f32[443648]{0:T(1024)} async-done(((f32[443648]{0:T(1024)}), f32[443648]{0:T(1024)}) %all-reduce.4.cloned.1.call-update) | async-done | bytes 1774608 | tf_op jit(solution)/shard_map/psum | solution.py:343
  1003.9 4.0 fusion.69
  (466 shorter events, 222.4 us)
Async XLA Ops:
  7.2 146.6 %all-gather.5.cloned.1.call-start = ((), (), s32[]{:S(2)}) async-start(), calls=%async_computation.2 | async-start | bytes 1966080 | tf_op jit(solution)/shard_map/all_gather | solution.py:250
  19.7 10.6 %collective-permute-start = (bf16[1,443648]{1,0:T(2,128)(2,1)}, bf16[1,443648]{1,0:T(2,128)(2,1)S(1)}, u32[]{:S(2)}, u32[]{:S(2)}) collective-permute-start(bf16[1,443648]{1,0:T(2,128)(2,1)} %broadcast_in_dim.13), channel_id=1, source_target_pairs={{0,8},{8,0},{16,24},{24,16},{1,9},{9,1},{17,25},{25,17},{2,10},{10... | collective-permute-start | bytes 2661896 | tf_op jit(solution)/shard_map/ppermute | solution.py:29
  41.9 8.3 copy-start.16
  47.7 42.0 %collective-permute-start.1 = (bf16[2,443648]{1,0:T(2,128)(2,1)S(1)}, bf16[2,443648]{1,0:T(2,128)(2,1)}, u32[]{:S(2)}, u32[]{:S(2)}) collective-permute-start(bf16[2,443648]{1,0:T(2,128)(2,1)S(1)} %bitcast.139), channel_id=1, source_target_pairs={{0,16},{8,24},{16,0},{24,8},{1,17},{9,25},{17,1},{25,9},{2,18},{10... | collective-permute-start | bytes 5323784 | tf_op jit(solution)/shard_map/ppermute | solution.py:29
  50.9 38.8 %copy-start.65 = (f32[2,256]{1,0:T(2,128)}, f32[2,256]{1,0:T(2,128)S(1)}, u32[]{:S(2)}) copy-start(f32[2,256]{1,0:T(2,128)S(1)} %get-tuple-element.357) | copy-start | bytes 6148
  105.7 9.1 copy-start.9
  110.3 18.7 %copy-start.61 = (f32[384]{0:T(512)}, f32[384]{0:T(512)S(1)}, u32[]{:S(2)}) copy-start(f32[384]{0:T(512)S(1)} %mul.385) | copy-start | bytes 4612
  116.8 15.6 %copy-start.7 = (f32[512,1152]{1,0:T(8,128)}, f32[512,1152]{1,0:T(8,128)S(1)}, u32[]{:S(2)}) copy-start(f32[512,1152]{1,0:T(8,128)S(1)} %convolution_add_fusion) | copy-start | bytes 7077892
  119.6 6.8 copy-start.10
  122.2 6.9 copy-start.55
  132.3 43.3 %all-gather.7.cloned.1.call-start = ((), (), s32[]{:S(2)}) async-start(), calls=%async_computation.3 | async-start | bytes 1966080 | tf_op jit(solution)/shard_map/all_gather | solution.py:251
  133.2 95.5 %all-gather.9.cloned.1.call-start = ((), (), s32[]{:S(2)}) async-start(), calls=%async_computation.6 | async-start | bytes 8872960 | tf_op jit(solution)/shard_map/all_gather | solution.py:265
  134.0 536.1 %reduce-scatter.7.cloned.1.call-start = ((), (), s32[]{:S(2)}) async-start(), calls=%async_computation.7 | async-start | bytes 1966080
  138.4 6.8 copy-start.63
  148.3 27.3 %copy-start.52 = (f32[2,256,384]{2,1,0:T(8,128)S(1)}, f32[2,256,384]{2,1,0:T(8,128)}, u32[]{:S(2)}) copy-start(f32[2,256,384]{2,1,0:T(8,128)} %custom-call) | copy-start | bytes 2359300
  175.6 19.3 %copy-start.17 = (bf16[2,256,384]{2,1,0:T(8,128)(2,1)S(1)}, bf16[2,256,384]{2,1,0:T(8,128)(2,1)}, u32[]{:S(2)}) copy-start(bf16[2,256,384]{2,1,0:T(8,128)(2,1)} %param.11) | copy-start | bytes 1179652
  175.6 19.4 %copy-start.45 = (bf16[384,384]{1,0:T(8,128)(2,1)S(1)}, bf16[384,384]{1,0:T(8,128)(2,1)}, u32[]{:S(2)}) copy-start(bf16[384,384]{1,0:T(8,128)(2,1)} %reshape.332) | copy-start | bytes 884740
  175.6 19.4 %copy-start.68 = (f32[384]{0:T(512)S(1)}, f32[384]{0:T(512)}, u32[]{:S(2)}) copy-start(f32[384]{0:T(512)} %get-tuple-element.340) | copy-start | bytes 4612
  195.7 133.0 %copy-start.22 = (f32[512,384]{1,0:T(8,128)}, f32[512,384]{1,0:T(8,128)S(1)}, u32[]{:S(2)}) copy-start(f32[512,384]{1,0:T(8,128)S(1)} %get-tuple-element.359) | copy-start | bytes 2359300
  195.9 132.7 %copy-start.75 = (f32[512]{0:T(512)}, f32[512]{0:T(512)S(1)}, u32[]{:S(2)}) copy-start(f32[512]{0:T(512)S(1)} %add_rsqrt_fusion.2) | copy-start | bytes 6148
  469.8 163.4 %copy-start.69 = (f32[1,2,2,128]{3,2,1,0:T(2,128)S(1)}, f32[1,2,2,128]{3,2,1,0:T(2,128)}, u32[]{:S(2)}) copy-start(f32[1,2,2,128]{3,2,1,0:T(2,128)} %get-tuple-element.356) | copy-start | bytes 6148
  469.8 164.0 %copy-start.70 = (f32[1,2,2,128]{3,2,1,0:T(2,128)S(1)}, f32[1,2,2,128]{3,2,1,0:T(2,128)}, u32[]{:S(2)}) copy-start(f32[1,2,2,128]{3,2,1,0:T(2,128)} %get-tuple-element.354) | copy-start | bytes 6148
  632.5 136.6 %reduce-scatter.5.cloned.1.call-start = ((), (), s32[]{:S(2)}) async-start(), calls=%async_computation.4 | async-start | bytes 1966080 | tf_op jit(solution)/shard_map/reduce_scatter | solution.py:296
  635.5 7.0 copy-start.2
  643.9 261.1 %all-reduce.6.cloned.1.call-start = ((), (), s32[]{:S(2)}) async-start(), calls=%async_computation.8 | async-start | bytes 7098368
  658.1 8.1 copy-start.13
  658.1 8.1 copy-start.58
  749.4 7.0 copy-start.11
  749.5 7.0 copy-start.56
  829.5 79.7 %copy-start.36 = (bf16[589824]{0:T(1024)(128)(2,1)S(1)}, bf16[589824]{0:T(1024)(128)(2,1)}, u32[]{:S(2)}) copy-start(bf16[589824]{0:T(1024)(128)(2,1)} %get-tuple-element.343) | copy-start | bytes 3538948
  829.5 174.4 %all-reduce.4.cloned.1.call-start = ((), (), s32[]{:S(2)}) async-start(), calls=%async_computation.5 | async-start | bytes 3555328 | tf_op jit(solution)/shard_map/psum | solution.py:343
  914.3 89.7 %copy-start.21 = (f32[443648]{0:T(1024)S(1)}, f32[443648]{0:T(1024)}, u32[]{:S(2)}) copy-start(f32[443648]{0:T(1024)} %param.13) | copy-start | bytes 5323780
  (103 other events, 279.0 us)
Sparse Core Ops, SparseCore 0:
  132.5 21.2 all-gather.4
  155.9 19.6 all-gather.6
  177.8 50.9 all-gather.8
  632.6 28.0 reduce-scatter.6
  663.7 27.9 reduce-scatter.4
  829.6 75.2 all-reduce.5
  909.2 94.7 all-reduce.3
